TPU v7x, 512 devices: a whole 4x8x8 slice. The times are simulated.
512 devices in a mesh: req: 32 (over z, y_lo), tp: 16 (over y_hi, x, core).
Axes of the slice: x: 4, y: 8 (y_hi: 2, y_lo: 4; y = y_hi * 4 + y_lo), z: 8, core: 2. Of those that a mesh axis runs over, the one named last changes fastest.
Arguments:
- tokens: bfloat16 [16384, 4096], P(('req', 'tp')), parts along dimension 0, may hold values from -400 to 400
- norm_gain: bfloat16 [4096], replicated, may hold values from 0.099609375 to 1.8984375
- qkv_weight: bfloat16 [4096, 6144], P(None, 'tp'), may hold values from -0.46875 to 0.46875
- out_weight: bfloat16 [2048, 4096], P('tp'), may hold values from -0.5 to 0.5
- segment_ids: int32 [16384], P('req'), parts along dimension 0, may hold values from 0 to 7, never falling along the last dimension, each value on 1 to 170 neighbouring positions
- prefix_pages: int32 [256], P('req'), parts along dimension 0, may hold values from 1 to 16, 48 in all
- page_order: int32 [1536], P('req'), parts along dimension 0, may hold values from 0 to 47, each once
- fresh_order: int32 [1280], P('req'), parts along dimension 0, may hold values from 0 to 39, each once
- cache_pool: bfloat16 [2, 16, 1536, 16, 128], P(None, 'tp', 'req'), parts along dimension 2, may hold values from -6 to 6
Outputs:
- attn_out: bfloat16 [16384, 4096], P(('req', 'tp')), parts along dimension 0
- fresh_pages: bfloat16 [2, 16, 1280, 16, 128], P(None, 'tp', 'req'), parts along dimension 2
There are 32 independent parts, one for each index of `req`. A program takes and returns all parts, laid end to end along the dimension named above; an argument that names none is the same for every part. Nothing has to cross between parts.
Inputs may be any that keep to these rules, and one draw needn't show every extreme that they name: `segment_ids`: segment numbers never fall; every prompt has at least one new token and one has exactly 170. `prefix_pages`: they sum to 48; the largest is 16. `page_order`: every page once. `fresh_order`: every page once.
All inputs are finite; a program needn't handle non-finite values.
Results may differ from a plain program's by a relative error of at most 0.014.
Values may be sent and summed in bfloat16 or wider, within the bound.
No kernel may reach another device: no remote copies, remote signals or barrier semaphores. Data moves between devices by JAX's collectives and lax.ppermute only.
A program may use at most 64 MiB of HBM per device.

v0:
```python
import jax
import jax.numpy as jnp
from jax import lax
from jax.sharding import PartitionSpec as P

MODEL_HEADS = 32


def layer_norm(values, gain):
    values = values.astype(jnp.float32)
    center = values - jnp.mean(values, axis=-1, keepdims=True)
    spread = jnp.mean(center * center, axis=-1, keepdims=True)
    return (center * lax.rsqrt(spread + 1e-05) * gain.astype(jnp.float32)).astype(jnp.bfloat16)


def token_layout(segment_ids, prefix_pages, page_order, fresh_order, page_len):
    seq_count = prefix_pages.shape[0]
    tok_count = segment_ids.shape[0]
    labels = jnp.arange(seq_count, dtype=jnp.int32)
    member = (segment_ids[:, None] == labels[None, :]).astype(jnp.int32)
    counts = jnp.sum(member, axis=0)
    starts = jnp.cumsum(counts) - counts
    token_index = jnp.arange(tok_count, dtype=jnp.int32)
    in_prompt = token_index - jnp.sum(member * starts[None, :], axis=1)
    prefix_len = prefix_pages * page_len
    position = in_prompt + jnp.sum(member * prefix_len[None, :], axis=1)
    fresh_counts = (counts + page_len - 1) // page_len
    fresh_starts = jnp.cumsum(fresh_counts) - fresh_counts
    page_slot = jnp.sum(member * fresh_starts[None, :], axis=1) + in_prompt // page_len
    target = jnp.take(fresh_order, page_slot) * page_len + in_prompt % page_len
    page_count = page_order.shape[0]
    cache_starts = jnp.cumsum(prefix_pages) - prefix_pages
    logical = (
        jnp.zeros((page_count,), jnp.int32)
        .at[page_order]
        .set(jnp.arange(page_count, dtype=jnp.int32))
    )
    holder = jnp.sum((logical[:, None] >= cache_starts[None, :]).astype(jnp.int32), axis=1) - 1
    holder_start = jnp.sum(
        (holder[:, None] == labels[None, :]).astype(jnp.int32) * cache_starts[None, :], axis=1
    )
    slot_index = jnp.arange(page_len, dtype=jnp.int32)
    key_owner = jnp.repeat(holder, page_len)
    key_pos = ((logical - holder_start)[:, None] * page_len + slot_index[None, :]).reshape(-1)
    return (in_prompt, position, target, key_owner, key_pos)


def attention_mask(segment_ids, in_prompt, position, key_owner, key_pos):
    cache_ok = segment_ids[:, None] == key_owner[None, :]
    new_ok = (segment_ids[:, None] == segment_ids[None, :]) & (
        in_prompt[None, :] <= in_prompt[:, None]
    )
    allowed = jnp.concatenate([cache_ok, new_ok], axis=1)
    key_all = jnp.concatenate([key_pos, position])
    distance = (position[:, None] - key_all[None, :]).astype(jnp.float32)
    return (allowed, distance)


def attend_head(queries, key_rows, values, alibi_slope, allowed, distance):
    scores = lax.dot_general(
        queries, key_rows, (((1,), (1,)), ((), ())), preferred_element_type=jnp.float32
    )
    scores = scores * queries.shape[1] ** (-0.5) - alibi_slope * distance
    scores = jnp.where(allowed, scores, -1e30)
    peak_score = jnp.max(scores, axis=1, keepdims=True)
    weights = jnp.exp(scores - peak_score)
    weights_bf = (weights / jnp.sum(weights, axis=1, keepdims=True)).astype(jnp.bfloat16)
    return jnp.dot(weights_bf, values, preferred_element_type=jnp.float32).astype(jnp.bfloat16)


def body(
    tokens,
    norm_gain,
    qkv_weight,
    out_weight,
    segment_ids,
    prefix_pages,
    page_order,
    fresh_order,
    cache_pool,
):
    head_dev = cache_pool.shape[1]
    page_len = cache_pool.shape[3]
    head_size = cache_pool.shape[4]
    tp_size = lax.axis_size("tp")
    first_head = lax.axis_index("tp") * head_dev
    normed = layer_norm(tokens, norm_gain)
    projected = jnp.dot(
        lax.all_gather(normed, "tp", axis=0, tiled=True),
        qkv_weight,
        preferred_element_type=jnp.float32,
    ).astype(jnp.bfloat16)
    tok_count = projected.shape[0]
    in_prompt, position, target, key_owner, key_pos = token_layout(
        segment_ids, prefix_pages, page_order, fresh_order, page_len
    )
    allowed, distance = attention_mask(segment_ids, in_prompt, position, key_owner, key_pos)
    per_head = projected.reshape(tok_count, head_dev, 3, head_size)
    step_heads = MODEL_HEADS // (head_dev * tp_size)
    alibi_slope = jnp.exp2(
        -8.0 * (first_head + 0 + 1).astype(jnp.float32) * step_heads / MODEL_HEADS
    )
    key_rows = jnp.concatenate([cache_pool[0, 0].reshape(-1, head_size), per_head[:, 0, 1]], axis=0)
    values = jnp.concatenate([cache_pool[1, 0].reshape(-1, head_size), per_head[:, 0, 2]], axis=0)
    contexts = attend_head(per_head[:, 0, 0], key_rows, values, alibi_slope, allowed, distance)
    summed = lax.psum_scatter(
        jnp.dot(contexts, out_weight, preferred_element_type=jnp.float32).astype(jnp.bfloat16),
        "tp",
        scatter_dimension=0,
        tiled=True,
    )
    fresh_total = fresh_order.shape[0]
    new_kv = per_head[:, :, 1:3].transpose(2, 1, 0, 3)
    fresh_pages = (
        jnp.zeros((2, head_dev, fresh_total * page_len, head_size), jnp.bfloat16)
        .at[:, :, target]
        .set(new_kv)
    )
    return (summed, fresh_pages.reshape(2, head_dev, fresh_total, page_len, head_size))


def solution(mesh):
    placed = (
        P(("req", "tp"), None),
        P(),
        P(None, "tp"),
        P("tp", None),
        P("req"),
        P("req"),
        P("req"),
        P("req"),
        P(None, "tp", "req", None, None),
    )
    return jax.shard_map(
        body,
        mesh=mesh,
        in_specs=placed,
        out_specs=(P(("req", "tp"), None), P(None, "tp", "req", None, None)),
        check_vma=False,
    )
```

profile of v0, /device:TPU:8, one launch (start us, length us, event | category | flops | bytes accessed | tf_op | source)
XLA Modules:
  0.0 233.2 jit_solution(15736835718099933660)
XLA Ops:
  7.2 1.2 convert_reduce_fusion
  8.5 1.2 fusion.7
  10.4 1.8 fusion.9
  12.3 0.8 convert_reduce_fusion.1
  13.5 0.8 reduce-window.25
  16.9 0.8 select_reduce_fusion
  17.7 1.7 compare_and_fusion
  19.4 1.7 broadcast_compare_fusion
  21.1 1.8 fusion.26
  22.9 75.8 %all-gather.2.cloned.1.call-done = bf16[512,4096]{1,0:T(8,128)(2,1)} async-done(((bf16[32,4096]{1,0:T(8,128)(2,1)}), bf16[512,4096]{1,0:T(8,128)(2,1)}) %all-gather.2.cloned.1.call-update) | async-done | bytes 4194320 | tf_op jit(solution)/shard_map/all_gather | solution.py:89
  98.8 4.0 %convolution_convert_fusion.1 = bf16[512,384]{0,1:T(8,128)(2,1)S(1)} fusion(bf16[512,4096]{1,0:T(8,128)(2,1)} %all-gather.2.cloned.1.call-done, bf16[4096,384]{1,0:T(8,128)(2,1)S(1)} %copy-done), kind=kOutput, calls=%fused_computation.10 | convolution fusion | flops 1610809344 | bytes 7733248 | tf_op jit(solution)/shard_map/dot_general | solution.py:88
  102.8 0.8 slice_bitcast_fusion
  103.6 1.7 copy.20
  105.3 1.7 copy.19
  106.9 2.3 %fusion.30 = (f32[512]{0:T(512)S(1)}, f32[512,1280]{1,0:T(8,128)S(1)}) fusion(s32[1280]{0:T(1024)S(1)} %pad_add_fusion, s32[512]{0:T(512)} %copy-done.6, f32[]{:T(128)S(6)} %exp2.7, bf16[512,128]{1,0:T(8,128)(2,1)} %copy.19, bf16[768,128]{1,0:T(8,128)(2,1)} %bitcast.83, bf16[512,1,3,128]{0,3,2,1:T(8,128)(2,1)S(1)} %bitcast.80, ...), kind=kOutput, calls=%fused_computation.117 | convolution fusion | flops 173669888 | bytes 3747844 | tf_op jit(solution)/shard_map/dot_general | solution.py:60
  109.3 1.5 copy-done.1
  111.3 6.3 %convolution_convert_fusion = bf16[512,4096]{1,0:T(8,128)(2,1)} fusion(bf16[128,4096]{1,0:T(8,128)(2,1)} %param.12, f32[512,1280]{1,0:T(8,128)} %copy-done.1, f32[512]{0:T(512)S(1)} %fusion.2, f32[512]{0:T(512)} %copy-done.7, bf16[512,128]{1,0:T(8,128)(2,1)S(1)} %copy-done.5, bf16[768,128]{1,0:T(8,128)(2,1)S(1)} %bitcast.82), kind=kOutput, calls=%fused_computation.2 | convolution fusion | flops 709427200 | bytes 8196096 | tf_op jit(solution)/shard_map/dot_general | solution.py:107
  120.4 4.5 %compare_select_fusion.2 = (s32[512,1]{0,1:T(1,128)S(1)}, s32[512,1]{0,1:T(1,128)S(1)}) fusion(s32[]{:T(128)} %bitcast.46, s32[]{:T(128)} %bitcast.47, s32[]{:T(128)} %bitcast.48, s32[]{:T(128)} %bitcast.49, s32[]{:T(128)} %bitcast.50, s32[]{:T(128)} %bitcast.52, s32[]{:T(128)} %bitcast.51, s32[512,1]{0,1:T(1,128)S(1)} %bitcast.87, s32[512,1]{0,1:T(1,128)S(1)} %bitcast.84), kind=kLoop, calls=%fused_computation.72 | loop fusion | flops 16384 | bytes 8220 | tf_op jit(solution)/shard_map/jit(_take)/gather | solution.py:30
  125.1 20.5 %select_select_fusion = s32[512]{0:T(512)S(1)} fusion(pred[512]{0:T(512)(128)(4,1)S(1)} %get-tuple-element.39, pred[512]{0:T(512)(128)(4,1)S(1)} %get-tuple-element.38, pred[512]{0:T(512)(128)(4,1)S(1)} %get-tuple-element.40, pred[512]{0:T(512)(128)(4,1)S(1)} %get-tuple-element.37, pred[512]{0:T(512)(128)(4,1)S(1)} %get-tuple-element.36, ...), kind=kLoop, calls=%fused_computation.89 | loop fusion | flops 16896 | bytes 21124 | tf_op jit(solution)/shard_map/jit(_take)/gather | solution.py:30
  145.7 1.0 slice.68
  146.7 0.9 copy.23
  147.7 29.9 %scatter_fusion = bf16[2,640,128]{2,0,1:T(2,128)(2,1)S(1)} fusion(bf16[2,640,128]{2,0,1:T(2,128)(2,1)S(1)} %broadcast.454, s32[512]{0:T(512)S(1)} %bitcast.86, bf16[512,2,128]{2,1,0:T(2,128)(2,1)} %bitcast.78), kind=kCustom, calls=%fused_computation.1 | custom fusion | bytes 788480 | tf_op jit(solution)/shard_map/scatter | solution.py:117
  177.6 0.8 copy.22
  178.3 48.1 %reduce-scatter.2.cloned.1.call-done = bf16[32,4096]{1,0:T(8,128)(2,1)} async-done(((bf16[512,4096]{1,0:T(8,128)(2,1)}), bf16[32,4096]{1,0:T(8,128)(2,1)}) %reduce-scatter.2.cloned.1.call-update) | async-done | bytes 262160 | tf_op jit(solution)/shard_map/reduce_scatter | solution.py:106
  (46 shorter events, 7.5 us)
Async XLA Ops:
  7.2 91.6 %copy-start = (bf16[4096,384]{1,0:T(8,128)(2,1)S(1)}, bf16[4096,384]{1,0:T(8,128)(2,1)}, u32[]{:S(2)}) copy-start(bf16[4096,384]{1,0:T(8,128)(2,1)} %param.11) | copy-start | bytes 9437188
  7.2 91.6 %all-gather.2.cloned.1.call-start = ((), (), s32[]{:S(2)}) async-start(), calls=%async_computation.1 | async-start | bytes 4456448 | tf_op jit(solution)/shard_map/all_gather | solution.py:89
  12.2 214.2 %reduce-scatter.2.cloned.1.call-start = ((), (), s32[]{:S(2)}) async-start(), calls=%async_computation.2 | async-start | bytes 4456448 | tf_op jit(solution)/shard_map/reduce_scatter | solution.py:106
  17.7 5.3 %copy-start.6 = (s32[512]{0:T(512)}, s32[512]{0:T(512)S(1)}, u32[]{:S(2)}) copy-start(s32[512]{0:T(512)S(1)} %get-tuple-element.50) | copy-start | bytes 6148
  102.8 6.4 %copy-start.3 = (bf16[512,384]{0,1:T(8,128)(2,1)}, bf16[512,384]{0,1:T(8,128)(2,1)S(1)}, u32[]{:S(2)}) copy-start(bf16[512,384]{0,1:T(8,128)(2,1)S(1)} %convolution_convert_fusion.1) | copy-start | bytes 1179652
  109.3 1.5 copy-start.1
  109.3 2.0 copy-start.7
  109.3 2.0 copy-start.4
  109.3 2.0 copy-start.5
  117.7 0.7 copy-start.2
Sparse Core Ops, SparseCore 0:
  12.3 86.4 all-gather.1
  117.8 108.5 reduce-scatter.1
where the time goes:
time: 236 us; the launch traced here: 233 us
  waiting for transfers between devices  124 us (53%)
  local copies, waits for them, and re-layouts  43.7 us (19%)
  other arithmetic  38.6 us (16%)
  between operations  14.3 us (6%)
  matrix products  12.7 us (5%)
    all_gather x1, waiting for transfers between devices, body(): lax.all_gather(normed, 'tp', axis=0, tiled=True)  75.8 us
    reduce_scatter x1, waiting for transfers between devices, body(): lax.psum_scatter(jnp.dot(contexts, out_weight, preferred_element_type=jnp...  48.1 us
    scatter x1, local copies, waits for them, and re-layouts, body(): fresh_pages = jnp.zeros((2, head_dev, fresh_total * page_len, head_size),...  29.9 us
    gather x3, other arithmetic, token_layout(): target = jnp.take(fresh_order, page_slot) * page_len + in_prompt % page_len  25.2 us
    dot_general x1, matrix products, body(): jnp.dot(contexts, out_weight, preferred_element_type=jnp.float32)  6.32 us
  transfers between devices with their start and end apart: 2, of which 2 were waited for; matrix products, arithmetic and copies ran while one was open for 30% of the time, Pallas kernels for 0%

commit v1 on v0

--- a/solution.py
+++ b/solution.py
@@ -86,7 +86,9 @@
     first_head = lax.axis_index("tp") * head_dev
     normed = layer_norm(tokens, norm_gain)
     projected = jnp.dot(
-        lax.all_gather(normed, "tp", axis=0, tiled=True),
+        jnp.concatenate(
+            lax.all_to_all(jnp.stack([normed] * lax.axis_size("tp")), "tp", 0, 0), axis=0
+        ),
         qkv_weight,
         preferred_element_type=jnp.float32,
     ).astype(jnp.bfloat16)

time: 236 us -> 273 us (1.16)
  waiting for transfers between devices: 124 us -> 145 us
  starting transfers between devices: 0.08 us -> 8.99 us
  local copies, waits for them, and re-layouts: 43.7 us -> 48.4 us
  other arithmetic: 38.6 us -> 41.4 us
    all_to_all x0 -> x1, waiting for transfers between devices: none -> 83.4 us  [body(): lax.all_to_all(jnp.stack([normed] * lax.axis_size('tp')), 'tp', 0, 0)]
    all_gather x1 -> x0, waiting for transfers between devices: 75.8 us -> none  [body(): lax.all_gather(normed, 'tp', axis=0, tiled=True)]
    reduce_scatter x1, waiting for transfers between devices: 48.1 us -> 61.5 us  [body(): lax.psum_scatter(jnp.dot(contexts, out_weight, preferred_element_type=jnp...]
    all_to_all x0 -> x1, starting transfers between devices: none -> 8.95 us  [body(): lax.all_to_all(jnp.stack([normed] * lax.axis_size('tp')), 'tp', 0, 0)]
  transfers between devices with their start and end apart: 2 -> 2, of which waited for: 2 -> 2; matrix products, arithmetic and copies ran while one was open for 30% -> 28% of each run, Pallas kernels for 0% -> 0%
where the time goes in v1:
time: 273 us; the launch traced here: 271 us
  waiting for transfers between devices  145 us (53%)
  local copies, waits for them, and re-layouts  48.4 us (18%)
  other arithmetic  41.4 us (15%)
  between operations  14.3 us (5%)
  matrix products  12.7 us (5%)
  starting transfers between devices  8.99 us (3%)
    all_to_all x1, waiting for transfers between devices, body(): lax.all_to_all(jnp.stack([normed] * lax.axis_size('tp')), 'tp', 0, 0)  83.4 us
    reduce_scatter x1, waiting for transfers between devices, body(): lax.psum_scatter(jnp.dot(contexts, out_weight, preferred_element_type=jnp...  61.5 us
    scatter x1, local copies, waits for them, and re-layouts, body(): fresh_pages = jnp.zeros((2, head_dev, fresh_total * page_len, head_size),...  29.9 us
    gather x3, other arithmetic, token_layout(): target = jnp.take(fresh_order, page_slot) * page_len + in_prompt % page_len  25.3 us
    all_to_all x1, starting transfers between devices, body(): lax.all_to_all(jnp.stack([normed] * lax.axis_size('tp')), 'tp', 0, 0)  8.95 us
    dot_general x1, matrix products, body(): jnp.dot(contexts, out_weight, preferred_element_type=jnp.float32)  6.31 us
  transfers between devices with their start and end apart: 2, of which 2 were waited for; matrix products, arithmetic and copies ran while one was open for 28% of the time, Pallas kernels for 0%

profile of v1, /device:TPU:8, one launch (start us, length us, event | category | flops | bytes accessed | tf_op | source)
XLA Modules:
  0.0 270.6 jit_solution(2698689334590110422)
XLA Ops:
  8.0 1.2 convert_reduce_fusion
  9.2 1.2 fusion.7
  10.4 1.1 fusion.9
  11.5 2.5 stack.2
  14.0 8.9 %all-to-all-start = ((bf16[16,32,4096]{2,1,0:T(8,128)(2,1)}), bf16[16,32,4096]{2,1,0:T(8,128)(2,1)}, u32[]{:S(2)}, u32[]{:S(2)}) async-start(bf16[16,32,4096]{2,1,0:T(8,128)(2,1)} %stack.2), calls=%async_computation | async-start | bytes 8388608 | tf_op jit(solution)/shard_map/all_to_all | solution.py:90
  23.9 1.3 reduce-window.27
  25.9 1.2 compare_select_fusion.11
  27.6 1.3 scatter_custom_fusion
  28.9 1.2 bitcast_subtract_fusion.1
  34.5 1.2 select_reduce_fusion
  36.3 1.0 compare_and_fusion
  37.3 1.1 broadcast_compare_fusion
  39.2 83.4 %all-to-all-done = bf16[16,32,4096]{2,1,0:T(8,128)(2,1)} async-done(((bf16[16,32,4096]{2,1,0:T(8,128)(2,1)}), bf16[16,32,4096]{2,1,0:T(8,128)(2,1)}, u32[]{:S(2)}, u32[]{:S(2)}) %all-to-all-start) | async-done | bytes 4194336 | tf_op jit(solution)/shard_map/all_to_all | solution.py:90
  122.6 4.0 %convolution_convert_fusion.1 = bf16[512,384]{0,1:T(8,128)(2,1)S(1)} fusion(bf16[512,4096]{1,0:T(8,128)(2,1)} %bitcast.4, bf16[4096,384]{1,0:T(8,128)(2,1)S(1)} %copy-done), kind=kOutput, calls=%fused_computation.10 | convolution fusion | flops 1610809344 | bytes 7733248 | tf_op jit(solution)/shard_map/dot_general | solution.py:88
  127.4 1.7 copy.19
  129.1 1.7 copy.20
  130.7 2.3 fusion.30
  133.1 1.5 copy-done.1
  135.2 6.3 %convolution_convert_fusion = bf16[512,4096]{1,0:T(8,128)(2,1)} fusion(bf16[128,4096]{1,0:T(8,128)(2,1)} %param.12, f32[512,1280]{1,0:T(8,128)} %copy-done.1, f32[512]{0:T(512)S(1)} %fusion.2, f32[512]{0:T(512)} %copy-done.12, bf16[512,128]{1,0:T(8,128)(2,1)S(1)} %copy-done.6, bf16[768,128]{1,0:T(8,128)(2,1)S(1)} %bitcast.81), kind=kOutput, calls=%fused_computation.2 | convolution fusion | flops 709427200 | bytes 8196096 | tf_op jit(solution)/shard_map/dot_general | solution.py:109
  144.2 4.4 %compare_select_fusion.2 = (s32[512,1]{0,1:T(1,128)S(1)}, s32[512,1]{0,1:T(1,128)S(1)}) fusion(s32[]{:T(128)} %bitcast.47, s32[]{:T(128)} %bitcast.48, s32[]{:T(128)} %bitcast.49, s32[]{:T(128)} %bitcast.50, s32[]{:T(128)} %bitcast.51, s32[]{:T(128)} %bitcast.53, s32[]{:T(128)} %bitcast.52, s32[512,1]{0,1:T(1,128)S(1)} %bitcast.86, s32[512,1]{0,1:T(1,128)S(1)} %bitcast.83), kind=kLoop, calls=%fused_computation.72 | loop fusion | flops 16384 | bytes 8220 | tf_op jit(solution)/shard_map/jit(_take)/gather | solution.py:30
  148.9 20.7 %select_select_fusion = s32[512]{0:T(512)S(1)} fusion(pred[512]{0:T(512)(128)(4,1)S(1)} %get-tuple-element.39, pred[512]{0:T(512)(128)(4,1)S(1)} %get-tuple-element.38, pred[512]{0:T(512)(128)(4,1)S(1)} %get-tuple-element.40, pred[512]{0:T(512)(128)(4,1)S(1)} %get-tuple-element.37, pred[512]{0:T(512)(128)(4,1)S(1)} %get-tuple-element.36, ...), kind=kLoop, calls=%fused_computation.89 | loop fusion | flops 16896 | bytes 21124 | tf_op jit(solution)/shard_map/jit(_take)/gather | solution.py:30
  169.6 1.0 slice.68
  171.6 29.9 %scatter_fusion = bf16[2,640,128]{2,0,1:T(2,128)(2,1)S(1)} fusion(bf16[2,640,128]{2,0,1:T(2,128)(2,1)S(1)} %broadcast.456, s32[512]{0:T(512)S(1)} %bitcast.85, bf16[512,2,128]{2,1,0:T(2,128)(2,1)} %bitcast.77), kind=kCustom, calls=%fused_computation.1 | custom fusion | bytes 788480 | tf_op jit(solution)/shard_map/scatter | solution.py:119
  202.3 61.5 %reduce-scatter.2.cloned.1.call-done = bf16[32,4096]{1,0:T(8,128)(2,1)} async-done(((bf16[512,4096]{1,0:T(8,128)(2,1)}), bf16[32,4096]{1,0:T(8,128)(2,1)}) %reduce-scatter.2.cloned.1.call-update) | async-done | bytes 262160 | tf_op jit(solution)/shard_map/reduce_scatter | solution.py:108
  (58 shorter events, 14.8 us)
Async XLA Ops:
  7.2 115.4 %copy-start = (bf16[4096,384]{1,0:T(8,128)(2,1)S(1)}, bf16[4096,384]{1,0:T(8,128)(2,1)}, u32[]{:S(2)}) copy-start(bf16[4096,384]{1,0:T(8,128)(2,1)} %param.11) | copy-start | bytes 9437188
  14.0 9.0 %copy-start.7 = (s32[512]{0:T(512)S(1)}, s32[512]{0:T(512)}, u32[]{:S(2)}) copy-start(s32[512]{0:T(512)} %param.13) | copy-start | bytes 6148
  14.0 11.2 %copy-start.13 = (s32[8]{0:T(128)S(1)}, s32[8]{0:T(128)}, u32[]{:S(2)}) copy-start(s32[8]{0:T(128)} %param.14) | copy-start | bytes 100
  14.0 24.4 %copy-start.4 = (bf16[2,1,48,16,128]{4,3,2,1,0:T(8,128)(2,1)S(1)}, bf16[2,1,48,16,128]{4,3,2,1,0:T(8,128)(2,1)}, u32[]{:S(2)}) copy-start(bf16[2,1,48,16,128]{4,3,2,1,0:T(8,128)(2,1)} %param.17) | copy-start | bytes 1179652
  14.0 108.5 %all-to-all-start = ((bf16[16,32,4096]{2,1,0:T(8,128)(2,1)}), bf16[16,32,4096]{2,1,0:T(8,128)(2,1)}, u32[]{:S(2)}, u32[]{:S(2)}) async-start(bf16[16,32,4096]{2,1,0:T(8,128)(2,1)} %stack.2), calls=%async_computation | async-start | bytes 8388608 | tf_op jit(solution)/shard_map/all_to_all | solution.py:90
  23.0 240.8 %reduce-scatter.2.cloned.1.call-start = ((), (), s32[]{:S(2)}) async-start(), calls=%async_computation.2 | async-start | bytes 4456448 | tf_op jit(solution)/shard_map/reduce_scatter | solution.py:108
  35.7 0.6 copy-start.10
  122.6 8.1 %copy-start.8 = (s32[1280]{0:T(1024)S(1)}, s32[1280]{0:T(1024)}, u32[]{:S(2)}) copy-start(s32[1280]{0:T(1024)} %pad_add_fusion) | copy-start | bytes 15364
  122.6 8.1 %copy-start.11 = (s32[512]{0:T(512)S(1)}, s32[512]{0:T(512)}, u32[]{:S(2)}) copy-start(s32[512]{0:T(512)} %copy-done.10) | copy-start | bytes 6148
  126.6 6.4 %copy-start.3 = (bf16[512,384]{0,1:T(8,128)(2,1)}, bf16[512,384]{0,1:T(8,128)(2,1)S(1)}, u32[]{:S(2)}) copy-start(bf16[512,384]{0,1:T(8,128)(2,1)S(1)} %convolution_convert_fusion.1) | copy-start | bytes 1179652
  133.1 1.5 copy-start.1
  133.1 2.1 copy-start.12
  133.1 2.0 copy-start.5
  133.1 2.0 copy-start.6
  141.5 0.7 copy-start.2
  141.5 2.8 %copy-start.9 = (s32[512]{0:T(512)S(1)}, s32[512]{0:T(512)}, u32[]{:S(2)}) copy-start(s32[512]{0:T(512)} %get-tuple-element.41) | copy-start | bytes 6148
Sparse Core Ops, SparseCore 0:
  141.6 122.1 reduce-scatter.1
